TPU v7x, 32 devices: a whole 2x2x4 slice. The times are simulated.
32 devices in a mesh: dp: 8 (over y, x, core), mp: 4 (over z).
Axes of the slice: x: 2, y: 2, z: 4, core: 2. Of those that a mesh axis runs over, the one named last changes fastest.
Arguments:
- tokens: bfloat16 [8192, 5120], P('dp'), may hold values from -6 to 6
- norm_gain: bfloat16 [5120], replicated, may hold values from 0.099609375 to 1.8984375
- w_query: bfloat16 [5120, 5120], P('dp', 'mp'), may hold values from -0.078125 to 0.078125
- b_query: bfloat16 [5120], P('mp'), may hold values from -3 to 3
- keyvalue_weight: bfloat16 [5120, 2, 1024], P('dp', None, 'mp'), may hold values from -0.078125 to 0.078125
- b_keyval: bfloat16 [2, 1024], P(None, 'mp'), may hold values from -3 to 3
- w_out: bfloat16 [5120, 5120], P('mp', 'dp'), may hold values from -0.5 to 0.5
- kv_pool: bfloat16 [2, 512, 64, 1024], P(None, 'dp', None, 'mp'), may hold values from -64 to 64
- page_owner: int32 [8, 16], replicated, may hold values from 0 to 7, as said below
- page_index: int32 [8, 16], replicated, may hold values from 0 to 63
- prefix_pages: int32 [8], replicated, may hold values from 10 to 16, as said below
- prompt_device: int32 [8], replicated, may hold values from 0 to 7, each once
Outputs:
- attn_out: bfloat16 [8192, 5120], P('dp', 'mp')
Inputs may be any that keep to these rules, and one draw needn't show every extreme that they name: `page_owner`: slots at or beyond a prompt's prefix_pages are unused. Of one prompt's used slots at most 2 name the same owner, and some prompt has exactly 2 used slots with one owner. `prefix_pages`: some prompt has 16 used slots.
All inputs are finite; a program needn't handle non-finite values.
Results may differ from a plain program's by a relative error of at most 0.014.
The roundings to bfloat16 on the way count: a program that leaves them out, or rounds other values in their place, can miss the bound.
Values may be sent and summed in bfloat16 or wider, within the bound.
A program may use at most 192 MiB of HBM per device.

v0:
```python
import jax
import jax.numpy as jnp
from jax import lax
from jax.sharding import PartitionSpec as P

HD = 128
CAP = 2
rope_theta = 1000000.0
norm_eps = 1e-06
masked_score = -1e30


def rms_normed(rows, norm_gain):
    values = rows.astype(jnp.float32)
    inverse = lax.rsqrt(jnp.mean(values * values, axis=-1, keepdims=True) + norm_eps)
    return (values * inverse * norm_gain.astype(jnp.float32)).astype(jnp.bfloat16)


def rotary(values, positions):
    half_dim = values.shape[-1] // 2
    frequency = rope_theta ** (-jnp.arange(half_dim, dtype=jnp.float32) * 2.0 / values.shape[-1])
    angles = positions.astype(jnp.float32)[:, None] * frequency[None, :]
    cosine = jnp.cos(angles)[:, None, :]
    sine_part = jnp.sin(angles)[:, None, :]
    front_half = values[..., :half_dim]
    back_half = values[..., half_dim:]
    return jnp.concatenate(
        [front_half * cosine - back_half * sine_part, back_half * cosine + front_half * sine_part],
        axis=-1,
    )


def shards(
    tokens,
    norm_gain,
    w_query,
    b_query,
    keyvalue_weight,
    b_keyval,
    w_out,
    kv_pool,
    page_owner,
    page_index,
    prefix_pages,
    prompt_device,
):
    groups = lax.axis_size("dp")
    my_group = lax.axis_index("dp")
    seq_rows = tokens.shape[0]
    width_kv = keyvalue_weight.shape[2]
    kv_local = width_kv // HD
    heads_local = w_query.shape[1] // HD
    per_group = heads_local // kv_local
    page_len = kv_pool.shape[2]
    max_pages = page_owner.shape[1]
    group_ids = jnp.arange(groups, dtype=jnp.int32)
    slot_prompt = jnp.sum(
        jnp.where(prompt_device[None, :] == group_ids[:, None], group_ids[None, :], 0), axis=1
    )
    owners_all = jnp.take(page_owner, slot_prompt, axis=0)
    index_all = jnp.take(page_index, slot_prompt, axis=0)
    length_all = jnp.take(prefix_pages, slot_prompt, axis=0)
    slot_ids = jnp.arange(max_pages, dtype=jnp.int32)
    places = jnp.arange(CAP, dtype=jnp.int32)
    used = slot_ids[None, :] < length_all[:, None]
    mine = used & (owners_all == my_group)
    rank = jnp.cumsum(mine.astype(jnp.int32), axis=1) - 1
    chosen = mine[:, None, :] & (rank[:, None, :] == places[None, :, None])
    send_index = jnp.sum(jnp.where(chosen, index_all[:, None, :], 0), axis=2)
    send_live = jnp.any(chosen, axis=2)
    outgoing = jnp.take(kv_pool, send_index.reshape(-1), axis=1).reshape(
        2, groups, CAP, page_len, width_kv
    )
    outgoing = jnp.where(send_live[None, :, :, None, None], outgoing, jnp.zeros((), outgoing.dtype))
    arrived = lax.all_to_all(outgoing, "dp", split_axis=1, concat_axis=1, tiled=True)
    my_owners = jnp.take(owners_all, my_group, axis=0)
    my_length = jnp.take(length_all, my_group, axis=0)
    my_used = slot_ids < my_length
    cached = arrived
    counts = jnp.sum(
        ((my_owners[None, :] == group_ids[:, None]) & my_used[None, :]).astype(jnp.int32), axis=1
    )
    page_live = (places[None, :] < counts[:, None]).reshape(-1)
    cached_count = page_live.shape[0]
    cached = cached.reshape(2, cached_count * page_len, kv_local, HD)
    key_live = jnp.repeat(page_live, page_len)
    normed = rms_normed(tokens, norm_gain)
    columns = normed
    query = jnp.dot(
        columns,
        lax.all_gather(w_query, "dp", axis=0, tiled=True),
        preferred_element_type=jnp.float32,
    )
    piece = lax.all_gather(keyvalue_weight, "dp", axis=0, tiled=True)
    columns = normed
    keyval = jnp.dot(
        columns, piece.reshape(piece.shape[0], 2 * width_kv), preferred_element_type=jnp.float32
    )
    query = query + b_query.astype(jnp.float32)
    keyval = keyval + b_keyval.reshape(2 * width_kv).astype(jnp.float32)
    row_ids = jnp.arange(seq_rows, dtype=jnp.int32)
    positions = my_length * page_len + row_ids
    rotated = rotary(query.reshape(seq_rows, heads_local, HD), positions).astype(jnp.bfloat16)
    new_keys = rotary(keyval[:, :width_kv].reshape(seq_rows, kv_local, HD), positions).astype(
        jnp.bfloat16
    )
    new_values = keyval[:, width_kv:].reshape(seq_rows, kv_local, HD).astype(jnp.bfloat16)
    gathered_keys = jnp.concatenate([cached[0], new_keys], axis=0)
    all_values = jnp.concatenate([cached[1], new_values], axis=0)
    scale = HD ** (-0.5)
    block = min(512, seq_rows)
    outputs = []
    for begin in range(0, seq_rows, block):
        query_block = rotated[begin : begin + block].reshape(block, kv_local, per_group, HD)
        logit_scores = (
            jnp.einsum(
                "qkgd,nkd->kgqn", query_block, gathered_keys, preferred_element_type=jnp.float32
            )
            * scale
        )
        causal = row_ids[None, :] <= (begin + jnp.arange(block, dtype=jnp.int32))[:, None]
        allowed = jnp.concatenate(
            [jnp.broadcast_to(key_live[None, :], (block, key_live.shape[0])), causal], axis=1
        )
        logit_scores = jnp.where(allowed[None, None], logit_scores, masked_score)
        top = jnp.max(logit_scores, axis=-1, keepdims=True)
        raised = jnp.exp(logit_scores - top)
        weights = (raised / jnp.sum(raised, axis=-1, keepdims=True)).astype(jnp.bfloat16)
        attended = jnp.einsum(
            "kgqn,nkd->qkgd", weights, all_values, preferred_element_type=jnp.float32
        ).astype(jnp.bfloat16)
        outputs.append(attended.reshape(block, heads_local * HD))
    attention = jnp.concatenate(outputs, axis=0)
    partial_out = jnp.dot(
        attention,
        lax.all_gather(w_out, "dp", axis=1, tiled=True),
        preferred_element_type=jnp.float32,
    )
    return lax.psum_scatter(partial_out.astype(jnp.bfloat16), "mp", scatter_dimension=1, tiled=True)


def solution(mesh):
    return jax.shard_map(
        shards,
        mesh=mesh,
        in_specs=(
            P("dp", None),
            P(),
            P("dp", "mp"),
            P("mp"),
            P("dp", None, "mp"),
            P(None, "mp"),
            P("mp", "dp"),
            P(None, "dp", None, "mp"),
            P(),
            P(),
            P(),
            P(),
        ),
        out_specs=P("dp", "mp"),
        check_vma=False,
    )
```

profile of v0, /device:TPU:0, one launch (start us, length us, event | category | flops | bytes accessed | tf_op | source)
XLA Modules:
  0.0 446.5 jit_solution(14333312355319830557)
XLA Ops:
  6.5 0.7 all-gather.4.cloned.1.call-update
  7.3 0.0 all-gather.6.cloned.1.call-start
  7.3 0.7 all-gather.6.cloned.1.call-update
  8.0 0.8 select_reduce_fusion.1
  8.8 1.3 gather_fusion
  10.1 0.6 gather_fusion.2
  10.7 1.2 gather_fusion.3
  11.9 0.1 fusion.45
  12.0 0.2 reduce_window_sum.11
  12.2 0.1 broadcast_select_fusion
  12.3 0.1 select_reduce_fusion
  12.4 0.1 copy.86
  12.5 0.1 reshape.210
  12.6 2.8 gather_fusion.1
  15.4 0.1 copy.87
  15.6 0.1 copy.85
  15.7 0.2 fusion.32
  15.8 0.1 copy.84
  15.9 0.2 select_select_fusion
  16.1 1.1 copy.88
  17.2 5.2 %all-to-all-start = ((bf16[2,8,2,64,256]{4,3,2,0,1:T(8,128)(2,1)}), bf16[2,8,2,64,256]{4,3,2,0,1:T(8,128)(2,1)S(1)}, u32[]{:S(2)}, u32[]{:S(2)}) async-start(bf16[2,8,2,64,256]{4,3,2,0,1:T(8,128)(2,1)} %copy.88), calls=%async_computation | async-start | bytes 2097152 | tf_op jit(solution)/shard_map/all_to_all | solution.py:75
  22.4 0.0 all-gather.8.cloned.1.call-start
  22.5 0.7 all-gather.8.cloned.1.call-update
  23.2 0.0 reduce-scatter.2.cloned.1.call-start
  23.2 0.6 dynamic-slice.6
  24.5 0.1 convert_reduce_fusion
  24.7 0.1 iota_compare_fusion.4
  24.7 0.1 lt.96
  24.8 0.1 broadcast_in_dim.145
  24.9 0.1 reshape.310
  25.0 1.0 multiply_cosine_fusion
  26.0 1.0 copy.91
  27.0 1.0 copy.93
  28.0 6.1 %fusion.4 = f32[1024]{0:T(1024)S(1)} fusion(bf16[1024,5120]{1,0:T(8,128)(2,1)} %param.14), kind=kLoop, calls=%fused_computation.16 | loop fusion | flops 15727616 | bytes 10489856 | tf_op jit(solution)/shard_map/reduce_sum | solution.py:15
  34.1 0.5 iota_compare_fusion
  34.6 2.7 pad_add_fusion
  37.3 4.1 all-to-all-done
  41.4 0.1 fusion.47
  41.5 0.1 squeeze.7
  41.6 0.9 copy.94
  42.5 0.1 squeeze.6
  42.6 1.1 copy.89
  43.7 18.7 %all-gather.4.cloned.1.call-done = bf16[5120,2,256]{2,1,0:T(2,128)(2,1)} async-done(((bf16[640,2,256]{2,1,0:T(2,128)(2,1)}), bf16[5120,2,256]{2,1,0:T(2,128)(2,1)}) %all-gather.4.cloned.1.call-update) | async-done | bytes 5242896 | tf_op jit(solution)/shard_map/all_gather | solution.py:94
  62.4 3.4 copy.106
  65.8 8.9 %fusion.27 = f32[1024,512]{0,1:T(8,128)S(1)} fusion(bf16[5120,512]{1,0:T(8,128)(2,1)S(1)} %bitcast.94, bf16[1024,5120]{1,0:T(8,128)(2,1)} %param.14, f32[5120]{0:T(1024)S(1)} %convert_element_type.65, f32[1024]{0:T(1024)S(1)} %add_rsqrt_fusion, f32[512]{0:T(512)S(1)} %bitcast.102), kind=kOutput, calls=%fused_computation.45 | convolution fusion | flops 5390204928 | bytes 17852416 | tf_op jit(solution)/shard_map/dot_general | solution.py:96
  74.7 0.1 slice.66
  74.8 0.9 slice.84
  75.7 0.1 fusion.48
  75.8 0.3 copy.104
  76.1 0.3 copy.105
  76.4 2.5 subtract_convert_fusion.1
  79.0 59.6 %all-gather.6.cloned.1.call-done = bf16[5120,1280]{1,0:T(8,128)(2,1)} async-done(((bf16[640,1280]{1,0:T(8,128)(2,1)}), bf16[5120,1280]{1,0:T(8,128)(2,1)}) %all-gather.6.cloned.1.call-update) | async-done | bytes 13107216 | tf_op jit(solution)/shard_map/all_gather | solution.py:91
  138.5 20.0 %convolution_add_fusion = f32[1024,1280]{1,0:T(8,128)} fusion(bf16[5120,1280]{1,0:T(8,128)(2,1)} %all-gather.6.cloned.1.call-done, bf16[1024,5120]{1,0:T(8,128)(2,1)} %param.14, f32[5120]{0:T(1024)S(1)} %convert_element_type.65, f32[1024]{0:T(1024)S(1)} %add_rsqrt_fusion, f32[1280]{0:T(1024)S(1)} %convert_element_type.72), kind=kOutput, calls=%fused_computation.28 | convolution fusion | flops 13444055040 | bytes 28865536 | tf_op jit(solution)/shard_map/dot_general | solution.py:89
  158.5 5.9 %copy.95 = f32[1024,1280]{0,1:T(8,128)} copy(f32[1024,1280]{1,0:T(8,128)} %convolution_add_fusion) | data formatting | bytes 10485760 | tf_op jit(solution)/shard_map/add | solution.py:99
  164.4 3.4 subtract_convert_fusion
  167.8 0.3 fusion.30
  168.1 0.8 copy-done.3
  168.9 22.1 %fusion.50 = (f32[2,5,512]{2,1,0:T(8,128)S(1)}, f32[2,5,512,2048]{2,3,1,0:T(8,128)}) fusion(pred[512,2048]{0,1:T(8,128)(4,1)} %get-tuple-element.45, bf16[512,2,5,128]{0,3,2,1:T(8,128)(2,1)S(1)} %bitcast.99, bf16[1024,2,64]{2,0,1:T(8,128)(2,1)} %get-tuple-element.36, bf16[1024,2,64]{2,0,1:T(8,128)(2,1)} %get-tuple-element.35, ...), kind=kOutput, calls=%fused_computation.102 | convolution fusion | flops 2729445376 | bytes 45371392 | tf_op jit(solution)/shard_map/sub | solution.py:127
  190.9 20.5 %fusion.49 = (f32[2,5,512]{2,1,0:T(8,128)S(1)}, f32[2,5,512,2048]{2,3,1,0:T(8,128)}) fusion(pred[512,2048]{0,1:T(8,128)(4,1)} %get-tuple-element.46, bf16[512,2,5,128]{0,3,2,1:T(8,128)(2,1)S(1)} %bitcast.98, bf16[1024,2,64]{2,0,1:T(8,128)(2,1)} %get-tuple-element.36, bf16[1024,2,64]{2,0,1:T(8,128)(2,1)} %get-tuple-element.35, ...), kind=kOutput, calls=%fused_computation.101 | convolution fusion | flops 2729445376 | bytes 45371392 | tf_op jit(solution)/shard_map/sub | solution.py:127
  211.4 14.7 %fusion.26 = bf16[2,128,5,512]{3,1,2,0:T(8,128)(2,1)S(1)} fusion(f32[2,5,512,2048]{2,3,1,0:T(8,128)} %get-tuple-element.51, f32[2,5,512]{2,1,0:T(8,128)S(1)} %get-tuple-element.50, bf16[1024,2,128]{0,2,1:T(8,128)(2,1)S(1)} %bitcast.100, bf16[1024,2,128]{0,2,1:T(8,128)(2,1)S(1)} %copy-done.2), kind=kOutput, calls=%fused_computation.44 | convolution fusion | flops 2708078592 | bytes 44322816 | tf_op jit(solution)/shard_map/kgqn,nkd->qkgd/dot_general | solution.py:129
  226.1 15.6 %fusion.25 = bf16[2,128,5,512]{3,1,2,0:T(8,128)(2,1)} fusion(f32[2,5,512,2048]{2,3,1,0:T(8,128)} %get-tuple-element.49, f32[2,5,512]{2,1,0:T(8,128)S(1)} %get-tuple-element.48, bf16[1024,2,128]{0,2,1:T(8,128)(2,1)S(1)} %bitcast.101, bf16[1024,2,128]{0,2,1:T(8,128)(2,1)S(1)} %copy-done.2), kind=kOutput, calls=%fused_computation.43 | convolution fusion | flops 2708078592 | bytes 44322816 | tf_op jit(solution)/shard_map/kgqn,nkd->qkgd/dot_general | solution.py:129
  241.7 19.7 %convolution_convert_fusion = bf16[1024,5120]{1,0:T(8,128)(2,1)} fusion(bf16[1280,5120]{1,0:T(8,128)(2,1)} %all-gather.8.cloned.1.call-done, bf16[512,1280]{0,1:T(8,128)(2,1)} %bitcast.104, bf16[512,1280]{0,1:T(8,128)(2,1)S(1)} %bitcast.103), kind=kOutput, calls=%fused_computation.27 | convolution fusion | flops 13432258560 | bytes 26214400 | tf_op jit(solution)/shard_map/dot_general | solution.py:134
  261.4 0.0 reduce-scatter.2.cloned.1.call-update
  261.5 178.5 %reduce-scatter.2.cloned.1.call-done = bf16[1024,1280]{1,0:T(8,128)(2,1)} async-done(((bf16[1024,5120]{1,0:T(8,128)(2,1)}), bf16[1024,1280]{1,0:T(8,128)(2,1)}) %reduce-scatter.2.cloned.1.call-update) | async-done | bytes 2621456 | tf_op jit(solution)/shard_map/reduce_scatter | solution.py:139
  (35 shorter events, 0.2 us)
Async XLA Ops:
  6.5 3.6 copy-start
  6.5 55.9 %all-gather.4.cloned.1.call-start = ((), (), s32[]{:S(2)}) async-start(), calls=%async_computation.2 | async-start | bytes 5898240 | tf_op jit(solution)/shard_map/all_gather | solution.py:94
  7.3 131.3 %all-gather.6.cloned.1.call-start = ((), (), s32[]{:S(2)}) async-start(), calls=%async_computation.3 | async-start | bytes 14745600 | tf_op jit(solution)/shard_map/all_gather | solution.py:91
  15.5 9.0 %copy-start.5 = (bf16[5120]{0:T(1024)(128)(2,1)S(1)}, bf16[5120]{0:T(1024)(128)(2,1)}, u32[]{:S(2)}) copy-start(bf16[5120]{0:T(1024)(128)(2,1)} %param.15) | copy-start | bytes 30724
  15.5 9.0 %copy-start.6 = (bf16[1280]{0:T(1024)(128)(2,1)S(1)}, bf16[1280]{0:T(1024)(128)(2,1)}, u32[]{:S(2)}) copy-start(bf16[1280]{0:T(1024)(128)(2,1)} %param.17) | copy-start | bytes 7684
  16.1 11.9 %copy-start.7 = (bf16[2,256]{1,0:T(2,128)(2,1)S(1)}, bf16[2,256]{1,0:T(2,128)(2,1)}, u32[]{:S(2)}) copy-start(bf16[2,256]{1,0:T(2,128)(2,1)} %param.19) | copy-start | bytes 3076
  17.2 24.1 %all-to-all-start = ((bf16[2,8,2,64,256]{4,3,2,0,1:T(8,128)(2,1)}), bf16[2,8,2,64,256]{4,3,2,0,1:T(8,128)(2,1)S(1)}, u32[]{:S(2)}, u32[]{:S(2)}) async-start(bf16[2,8,2,64,256]{4,3,2,0,1:T(8,128)(2,1)} %copy.88), calls=%async_computation | async-start | bytes 2097152 | tf_op jit(solution)/shard_map/all_to_all | solution.py:75
  22.4 219.3 %all-gather.8.cloned.1.call-start = ((), (), s32[]{:S(2)}) async-start(), calls=%async_computation.4 | async-start | bytes 14745600 | tf_op jit(solution)/shard_map/all_gather | solution.py:136
  23.2 416.8 %reduce-scatter.2.cloned.1.call-start = ((), (), s32[]{:S(2)}) async-start(), calls=%async_computation.5 | async-start | bytes 13107200 | tf_op jit(solution)/shard_map/reduce_scatter | solution.py:139
  167.8 1.0 copy-start.3
  190.9 20.5 %copy-start.2 = (bf16[1024,2,128]{0,2,1:T(8,128)(2,1)S(1)}, bf16[1024,2,128]{0,2,1:T(8,128)(2,1)}, u32[]{:S(2)}) copy-start(bf16[1024,2,128]{0,2,1:T(8,128)(2,1)} %copy.89) | copy-start | bytes 1572868
  190.9 20.5 %copy-start.4 = (bf16[1024,256]{0,1:T(8,128)(2,1)S(1)}, bf16[1024,256]{0,1:T(8,128)(2,1)}, u32[]{:S(2)}) copy-start(bf16[1024,256]{0,1:T(8,128)(2,1)} %slice.84) | copy-start | bytes 1572868
  261.4 178.6 %copy-start.1 = (s32[8,16]{1,0:T(8,128)S(1)}, s32[8,16]{1,0:T(8,128)}, u32[]{:S(2)}) copy-start(s32[8,16]{1,0:T(8,128)} %param.22) | copy-start | bytes 1540
Sparse Core Ops, SparseCore 0:
  9.2 53.1 all-gather.3
  64.3 74.1 all-gather.5
  140.4 74.0 all-gather.7
  261.6 178.3 reduce-scatter.1
where the time goes:
time: 447 us
  waiting for transfers between devices  263 us (59%)
  matrix products  121 us (27%)
  local copies, waits for them, and re-layouts  24.4 us (5%)
  other arithmetic  18.4 us (4%)
  between operations  14.1 us (3%)
  starting transfers between devices  5.31 us (1%)
    reduce_scatter x1, waiting for transfers between devices, shards(): lax.psum_scatter(partial_out.astype(jnp.bfloat16), 'mp', scatter_dimensio...  179 us
    all_gather x1, waiting for transfers between devices, shards(): lax.all_gather(w_query, 'dp', axis=0, tiled=True)  59.6 us
    sub x2, matrix products, shards(): raised = jnp.exp(logit_scores - top)  42.5 us
    dot_general x2, matrix products, shards(): jnp.einsum('kgqn,nkd->qkgd', weights, all_values, preferred_element_type=...  30.3 us
    dot_general x1, matrix products, shards(): jnp.dot(columns, lax.all_gather(w_query, 'dp', axis=0, tiled=True), prefe...  20 us
    dot_general x1, matrix products, shards(): jnp.dot(attention, lax.all_gather(w_out, 'dp', axis=1, tiled=True), prefe...  19.7 us
    all_gather x1, waiting for transfers between devices, shards(): piece = lax.all_gather(keyvalue_weight, 'dp', axis=0, tiled=True)  18.7 us
  transfers between devices with their start and end apart: 5, of which 4 were waited for; matrix products, arithmetic and copies ran while one was open for 32% of the time, Pallas kernels for 0%

commit v1 on v0

--- a/solution.py
+++ b/solution.py
@@ -8,6 +8,18 @@
 rope_theta = 1000000.0
 norm_eps = 1e-06
 masked_score = -1e30
+
+
+def gather_by_bits(value, axis, dim):
+    ways, here = (lax.axis_size(axis), lax.axis_index(axis))
+    grown, reach = (value, 1)
+    while reach < ways:
+        theirs = lax.ppermute(grown, axis, [(d, d ^ reach) for d in range(ways)])
+        mine_first = jnp.concatenate([grown, theirs], axis=dim)
+        theirs_first = jnp.concatenate([theirs, grown], axis=dim)
+        grown = jnp.where(here & reach == 0, mine_first, theirs_first)
+        reach = 2 * reach
+    return grown
 
 
 def rms_normed(rows, norm_gain):
@@ -86,11 +98,7 @@
     key_live = jnp.repeat(page_live, page_len)
     normed = rms_normed(tokens, norm_gain)
     columns = normed
-    query = jnp.dot(
-        columns,
-        lax.all_gather(w_query, "dp", axis=0, tiled=True),
-        preferred_element_type=jnp.float32,
-    )
+    query = jnp.dot(columns, gather_by_bits(w_query, "dp", 0), preferred_element_type=jnp.float32)
     piece = lax.all_gather(keyvalue_weight, "dp", axis=0, tiled=True)
     columns = normed
     keyval = jnp.dot(

time: 447 us -> 654 us (1.46)
  waiting for transfers between devices: 263 us -> 456 us
  other arithmetic: 18.4 us -> 29.4 us
    all_to_all x1, waiting for transfers between devices: 4.06 us -> 182 us  [shards(): lax.all_to_all(outgoing, 'dp', split_axis=1, concat_axis=1, tiled=True)]
    ppermute x0 -> x3, waiting for transfers between devices: none -> 93.6 us  [gather_by_bits(): theirs = lax.ppermute(grown, axis, [(d, d ^ reach) for d in range(ways)])]
    all_gather x1 -> x0, waiting for transfers between devices: 59.6 us -> none  [shards(): lax.all_gather(w_query, 'dp', axis=0, tiled=True)]
    all_gather x1, waiting for transfers between devices: 18.7 us -> 0.01 us  [shards(): piece = lax.all_gather(keyvalue_weight, 'dp', axis=0, tiled=True)]
    select_n x0 -> x2, other arithmetic: none -> 11.6 us  [gather_by_bits(): grown = jnp.where(here & reach == 0, mine_first, theirs_first)]
  transfers between devices with their start and end apart: 5 -> 7, of which waited for: 4 -> 4; matrix products, arithmetic and copies ran while one was open for 32% -> 24% of each run, Pallas kernels for 0% -> 0%
where the time goes in v1:
time: 654 us
  waiting for transfers between devices  456 us (70%)
  matrix products  123 us (19%)
  other arithmetic  29.4 us (4%)
  local copies, waits for them, and re-layouts  22.3 us (3%)
  between operations  14.1 us (2%)
  starting transfers between devices  8.91 us (1%)
    all_to_all x1, waiting for transfers between devices, shards(): lax.all_to_all(outgoing, 'dp', split_axis=1, concat_axis=1, tiled=True)  182 us
    reduce_scatter x1, waiting for transfers between devices, shards(): lax.psum_scatter(partial_out.astype(jnp.bfloat16), 'mp', scatter_dimensio...  179 us
    ppermute x3, waiting for transfers between devices, gather_by_bits(): theirs = lax.ppermute(grown, axis, [(d, d ^ reach) for d in range(ways)])  93.6 us
    sub x2, matrix products, shards(): raised = jnp.exp(logit_scores - top)  41.1 us
    dot_general x2, matrix products, shards(): jnp.einsum('kgqn,nkd->qkgd', weights, all_values, preferred_element_type=...  30.2 us
    dot_general x1, matrix products, shards(): jnp.dot(columns, gather_by_bits(w_query, 'dp', 0), preferred_element_type...  23.2 us
    dot_general x1, matrix products, shards(): jnp.dot(attention, lax.all_gather(w_out, 'dp', axis=1, tiled=True), prefe...  19.7 us
  transfers between devices with their start and end apart: 7, of which 4 were waited for; matrix products, arithmetic and copies ran while one was open for 24% of the time, Pallas kernels for 0%

profile of v1, /device:TPU:0, one launch (start us, length us, event | category | flops | bytes accessed | tf_op | source)
XLA Modules:
  0.0 653.6 jit_solution(6211342530754233766)
XLA Ops:
  6.6 0.7 all-gather.3.cloned.1.call-update
  7.3 0.6 collective-permute-start
  7.8 3.5 collective-permute-done
  11.3 3.4 maximum_select_fusion.5
  14.7 2.9 collective-permute-start.1
  17.7 0.1 select_reduce_fusion.1
  17.8 0.6 gather_fusion
  18.5 0.6 gather_fusion.2
  19.0 0.1 fusion.54
  19.1 0.2 reduce_window_sum.11
  19.3 0.6 gather_fusion.3
  19.8 0.1 broadcast_select_fusion
  19.9 90.1 %collective-permute-done.1 = bf16[1280,1280]{1,0:T(8,128)(2,1)} collective-permute-done((bf16[1280,1280]{1,0:T(8,128)(2,1)S(1)}, bf16[1280,1280]{1,0:T(8,128)(2,1)}, u32[]{:S(2)}, u32[]{:S(2)}) %collective-permute-start.1) | collective-permute-done | bytes 3276832 | tf_op jit(solution)/shard_map/ppermute | solution.py:17
  110.0 8.2 %maximum_select_fusion.2 = bf16[2560,1280]{1,0:T(8,128)(2,1)} fusion(bf16[1280,1280]{1,0:T(8,128)(2,1)} %collective-permute-done.1, bf16[1280,1280]{1,0:T(8,128)(2,1)S(1)} %maximum_select_fusion.5, pred[]{:T(512)S(6)} %eq.66), kind=kLoop, calls=%fused_computation.36 | loop fusion | flops 29491200 | bytes 13107201 | tf_op jit(solution)/shard_map/jit(_where)/select_n | solution.py:20
  118.2 1.8 collective-permute-start.2
  120.0 0.1 select_reduce_fusion
  120.1 0.1 copy.86
  120.2 0.1 reshape.210
  120.3 2.8 gather_fusion.1
  123.2 0.1 copy.87
  123.3 0.1 copy.85
  123.4 0.1 fusion.40
  123.5 0.1 copy.84
  123.6 0.2 select_select_fusion
  123.8 1.1 copy.88
  124.9 3.6 all-to-all-start
  128.5 0.0 all-gather.5.cloned.1.call-start
  128.5 0.7 all-gather.5.cloned.1.call-update
  129.3 0.6 dynamic-slice.6
  130.6 0.1 convert_reduce_fusion
  130.7 1.0 multiply_cosine_fusion
  131.7 6.1 fusion.4
  137.8 0.1 iota_compare_fusion.4
  137.9 0.1 lt.96
  138.0 0.1 broadcast_in_dim.145
  138.1 0.1 reshape.310
  138.2 1.0 copy.91
  139.2 1.0 copy.93
  140.2 0.5 iota_compare_fusion
  140.7 2.7 pad_add_fusion
  143.4 181.5 %all-to-all-done = bf16[2,8,2,64,256]{4,3,2,0,1:T(8,128)(2,1)S(1)} async-done(((bf16[2,8,2,64,256]{4,3,2,0,1:T(8,128)(2,1)}), bf16[2,8,2,64,256]{4,3,2,0,1:T(8,128)(2,1)S(1)}, u32[]{:S(2)}, u32[]{:S(2)}) %all-to-all-start) | async-done | bytes 1048608 | tf_op jit(solution)/shard_map/all_to_all | solution.py:87
  324.9 0.1 fusion.56
  325.0 0.1 squeeze.7
  325.2 0.9 copy.94
  326.0 0.1 squeeze.6
  326.2 1.1 copy.89
  327.3 3.4 copy.106
  330.6 8.9 %fusion.35 = f32[1024,512]{0,1:T(8,128)S(1)} fusion(bf16[5120,512]{1,0:T(8,128)(2,1)S(1)} %bitcast.93, bf16[1024,5120]{1,0:T(8,128)(2,1)} %param.14, f32[5120]{0:T(1024)S(1)} %convert_element_type.65, f32[1024]{0:T(1024)S(1)} %add_rsqrt_fusion, f32[512]{0:T(512)S(1)} %bitcast.101), kind=kOutput, calls=%fused_computation.55 | convolution fusion | flops 5390204928 | bytes 17852416 | tf_op jit(solution)/shard_map/dot_general | solution.py:104
  339.6 0.1 slice.66
  339.7 0.9 slice.84
  340.5 0.1 fusion.57
  340.6 0.3 copy.104
  340.9 0.3 copy.105
  341.3 2.5 subtract_convert_fusion.1
  343.8 23.2 %fusion.22 = f32[1024,1280]{1,0:T(8,128)} fusion(bf16[2560,1280]{1,0:T(8,128)(2,1)} %collective-permute-done.2, bf16[2560,1280]{1,0:T(8,128)(2,1)} %maximum_select_fusion.2, pred[]{:T(512)S(6)} %eq.65, bf16[1024,5120]{1,0:T(8,128)(2,1)} %param.14, f32[5120]{0:T(1024)S(1)} %convert_element_type.65, f32[1024]{0:T(1024)S(1)} %add_rsqrt_fusion, ...), kind=kOutput, calls=%fused_computation.37 | convolution fusion | flops 13503037440 | bytes 28865536 | tf_op jit(solution)/shard_map/dot_general | solution.py:101
  367.0 5.9 copy.95
  372.9 3.5 subtract_convert_fusion
  376.4 0.3 fusion.38
  376.7 20.6 %fusion.59 = (f32[2,5,512]{2,1,0:T(8,128)S(1)}, f32[2,5,512,2048]{2,3,1,0:T(8,128)}) fusion(pred[512,2048]{0,1:T(8,128)(4,1)} %get-tuple-element.45, bf16[512,2,5,128]{0,3,2,1:T(8,128)(2,1)S(1)} %bitcast.98, bf16[1024,2,64]{2,0,1:T(8,128)(2,1)} %get-tuple-element.36, bf16[1024,2,64]{2,0,1:T(8,128)(2,1)} %get-tuple-element.35, ...), kind=kOutput, calls=%fused_computation.113 | convolution fusion | flops 2729445376 | bytes 45371392 | tf_op jit(solution)/shard_map/sub | solution.py:135
  397.3 20.4 %fusion.58 = (f32[2,5,512]{2,1,0:T(8,128)S(1)}, f32[2,5,512,2048]{2,3,1,0:T(8,128)}) fusion(pred[512,2048]{0,1:T(8,128)(4,1)} %get-tuple-element.46, bf16[512,2,5,128]{0,3,2,1:T(8,128)(2,1)S(1)} %bitcast.97, bf16[1024,2,64]{2,0,1:T(8,128)(2,1)} %get-tuple-element.36, bf16[1024,2,64]{2,0,1:T(8,128)(2,1)} %get-tuple-element.35, ...), kind=kOutput, calls=%fused_computation.112 | convolution fusion | flops 2729445376 | bytes 45371392 | tf_op jit(solution)/shard_map/sub | solution.py:135
  417.8 14.6 %fusion.34 = bf16[2,128,5,512]{3,1,2,0:T(8,128)(2,1)S(1)} fusion(f32[2,5,512,2048]{2,3,1,0:T(8,128)} %get-tuple-element.51, f32[2,5,512]{2,1,0:T(8,128)S(1)} %get-tuple-element.50, bf16[1024,2,128]{0,2,1:T(8,128)(2,1)S(1)} %bitcast.99, bf16[1024,2,128]{0,2,1:T(8,128)(2,1)S(1)} %copy-done.3), kind=kOutput, calls=%fused_computation.54 | convolution fusion | flops 2708078592 | bytes 44322816 | tf_op jit(solution)/shard_map/kgqn,nkd->qkgd/dot_general | solution.py:137
  432.3 15.6 %fusion.33 = bf16[2,128,5,512]{3,1,2,0:T(8,128)(2,1)} fusion(f32[2,5,512,2048]{2,3,1,0:T(8,128)} %get-tuple-element.49, f32[2,5,512]{2,1,0:T(8,128)S(1)} %get-tuple-element.48, bf16[1024,2,128]{0,2,1:T(8,128)(2,1)S(1)} %bitcast.100, bf16[1024,2,128]{0,2,1:T(8,128)(2,1)S(1)} %copy-done.3), kind=kOutput, calls=%fused_computation.53 | convolution fusion | flops 2708078592 | bytes 44322816 | tf_op jit(solution)/shard_map/kgqn,nkd->qkgd/dot_general | solution.py:137
  447.9 19.7 %convolution_convert_fusion = bf16[1024,5120]{1,0:T(8,128)(2,1)} fusion(bf16[1280,5120]{1,0:T(8,128)(2,1)} %all-gather.5.cloned.1.call-done, bf16[512,1280]{0,1:T(8,128)(2,1)} %bitcast.103, bf16[512,1280]{0,1:T(8,128)(2,1)S(1)} %bitcast.102), kind=kOutput, calls=%fused_computation.35 | convolution fusion | flops 13432258560 | bytes 26214400 | tf_op jit(solution)/shard_map/dot_general | solution.py:142
  467.7 179.4 %reduce-scatter.2.cloned.1.call-done = bf16[1024,1280]{1,0:T(8,128)(2,1)} async-done(((bf16[1024,5120]{1,0:T(8,128)(2,1)}), bf16[1024,1280]{1,0:T(8,128)(2,1)}) %reduce-scatter.2.cloned.1.call-update) | async-done | bytes 2621456 | tf_op jit(solution)/shard_map/reduce_scatter | solution.py:147
  (47 shorter events, 0.3 us)
Async XLA Ops:
  6.5 11.9 %copy-start = (s32[8,16]{1,0:T(8,128)S(1)}, s32[8,16]{1,0:T(8,128)}, u32[]{:S(2)}) copy-start(s32[8,16]{1,0:T(8,128)} %param.22) | copy-start | bytes 1540
  6.5 11.1 %copy-start.10 = (s32[8]{0:T(128)S(1)}, s32[8]{0:T(128)}, u32[]{:S(2)}) copy-start(s32[8]{0:T(128)} %param.25) | copy-start | bytes 100
  6.5 11.2 %copy-start.2 = (s32[8]{0:T(128)S(1)}, s32[8]{0:T(128)}, u32[]{:S(2)}) copy-start(s32[8]{0:T(128)} %param.24) | copy-start | bytes 100
  6.5 12.7 %copy-start.6 = (s32[8,16]{1,0:T(8,128)S(1)}, s32[8,16]{1,0:T(8,128)}, u32[]{:S(2)}) copy-start(s32[8,16]{1,0:T(8,128)} %param.23) | copy-start | bytes 1540
  6.5 320.7 %all-gather.3.cloned.1.call-start = ((), (), s32[]{:S(2)}) async-start(), calls=%async_computation.2 | async-start | bytes 5898240 | tf_op jit(solution)/shard_map/all_gather | solution.py:102
  7.3 4.0 collective-permute-start
  14.7 95.3 %collective-permute-start.1 = (bf16[1280,1280]{1,0:T(8,128)(2,1)S(1)}, bf16[1280,1280]{1,0:T(8,128)(2,1)}, u32[]{:S(2)}, u32[]{:S(2)}) collective-permute-start(bf16[1280,1280]{1,0:T(8,128)(2,1)S(1)} %maximum_select_fusion.5), channel_id=1, source_target_pairs={{0,8},{4,12},{8,0},{12,4},{16,24},{20,28},{24,16},{28,20},{1,9},{5... | collective-permute-start | bytes 9830408 | tf_op jit(solution)/shard_map/ppermute | solution.py:17
  118.2 225.6 %collective-permute-start.2 = (bf16[2560,1280]{1,0:T(8,128)(2,1)}, bf16[2560,1280]{1,0:T(8,128)(2,1)}, u32[]{:S(2)}, u32[]{:S(2)}) collective-permute-start(bf16[2560,1280]{1,0:T(8,128)(2,1)} %maximum_select_fusion.2), channel_id=1, source_target_pairs={{0,16},{4,20},{8,24},{12,28},{16,0},{20,4},{24,8},{28,12},{1,17},{... | collective-permute-start | bytes 19660808 | tf_op jit(solution)/shard_map/ppermute | solution.py:17
  123.1 7.6 %copy-start.9 = (bf16[2,256]{1,0:T(2,128)(2,1)S(1)}, bf16[2,256]{1,0:T(2,128)(2,1)}, u32[]{:S(2)}) copy-start(bf16[2,256]{1,0:T(2,128)(2,1)} %param.19) | copy-start | bytes 3076
  124.9 200.0 %all-to-all-start = ((bf16[2,8,2,64,256]{4,3,2,0,1:T(8,128)(2,1)}), bf16[2,8,2,64,256]{4,3,2,0,1:T(8,128)(2,1)S(1)}, u32[]{:S(2)}, u32[]{:S(2)}) async-start(bf16[2,8,2,64,256]{4,3,2,0,1:T(8,128)(2,1)} %copy.88), calls=%async_computation | async-start | bytes 2097152 | tf_op jit(solution)/shard_map/all_to_all | solution.py:87
  128.5 319.4 %all-gather.5.cloned.1.call-start = ((), (), s32[]{:S(2)}) async-start(), calls=%async_computation.3 | async-start | bytes 14745600 | tf_op jit(solution)/shard_map/all_gather | solution.py:144
  129.2 517.9 %reduce-scatter.2.cloned.1.call-start = ((), (), s32[]{:S(2)}) async-start(), calls=%async_computation.4 | async-start | bytes 13107200 | tf_op jit(solution)/shard_map/reduce_scatter | solution.py:147
  131.7 6.2 copy-start.7
  131.7 6.2 copy-start.8
  372.9 3.8 copy-start.4
  397.3 20.4 %copy-start.3 = (bf16[1024,2,128]{0,2,1:T(8,128)(2,1)S(1)}, bf16[1024,2,128]{0,2,1:T(8,128)(2,1)}, u32[]{:S(2)}) copy-start(bf16[1024,2,128]{0,2,1:T(8,128)(2,1)} %copy.89) | copy-start | bytes 1572868
  397.3 20.4 %copy-start.5 = (bf16[1024,256]{0,1:T(8,128)(2,1)S(1)}, bf16[1024,256]{0,1:T(8,128)(2,1)}, u32[]{:S(2)}) copy-start(bf16[1024,256]{0,1:T(8,128)(2,1)} %slice.84) | copy-start | bytes 1572868
  467.7 179.4 %copy-start.1 = (s32[8,16]{1,0:T(8,128)S(1)}, s32[8,16]{1,0:T(8,128)}, u32[]{:S(2)}) copy-start(s32[8,16]{1,0:T(8,128)} %param.22) | copy-start | bytes 1540
Sparse Core Ops, SparseCore 0:
  9.2 64.4 all-gather.2
  131.2 128.5 all-gather.4
  467.8 179.2 reduce-scatter.1
